TPU v7x, 512 devices: a whole 4x8x8 slice. The times are simulated.
512 devices in a mesh: ka: 32 (over x, z), ba: 16 (over y, core).
Axes of the slice: x: 4, y: 8, z: 8, core: 2. Of those that a mesh axis runs over, the one named last changes fastest.
Arguments:
- density: float32 [2, 8192, 4096], P(None, 'ka', 'ba'), may hold values from -6 to 6
- h_bands: float32 [2, 8192, 4096], P(None, ('ka', 'ba')), may hold values from -0.75 to 0.75
- coupling: bfloat16 [64, 4, 128, 128], P('ka'), may hold values from -0.03125 to 0.03125
- donors: int32 [64, 4], P('ka'), may hold values from 0 to 63, as said below
- counts: int32 [64], P('ka'), may hold values from 2 to 4, as said below
Outputs:
- evolved: float32 [2, 8192, 4096], P(None, 'ka', 'ba')
Inputs may be any that keep to these rules, and one draw needn't show every extreme that they name: donors[t] holds 4 different tiles, each within 2 tiles of t in the cyclic order of the 64 tiles; donors[t, 0] = t. `counts`: some tile uses all 4 slots.
All inputs are finite; a program needn't handle non-finite values.
Results may differ from a plain program's by a relative error of at most 0.0013.
Values may be sent and summed in bfloat16 or wider, within the bound.
A program may use at most 64 MiB of HBM per device.

v0:
```python
import jax
import jax.numpy as jnp
from jax import lax
from jax.sharding import PartitionSpec as P

NB = 64
TILE = 128
ND = 4
REACH = 2


step_size = 0.25


def with_halo(cells, sides, width):
    for axis, dim in sides:
        count = lax.axis_size(axis)
        head = lax.slice_in_dim(cells, 0, width, axis=dim)
        tail = lax.slice_in_dim(cells, cells.shape[dim] - width, cells.shape[dim], axis=dim)
        cells = jnp.concatenate(
            [
                lax.ppermute(tail, axis, [(i, (i + 1) % count) for i in range(count)]),
                cells,
                lax.ppermute(head, axis, [((i + 1) % count, i) for i in range(count)]),
            ],
            axis=dim,
        )
    return cells


def commute(hamilton, state):
    count = state.shape[1]
    h_real = hamilton[0].reshape(count, NB, NB)
    h_imag = hamilton[1].reshape(count, NB, NB)
    s_real = state[0].reshape(count, NB, NB)
    s_imag = state[1].reshape(count, NB, NB)

    def product(left, right):
        return jnp.einsum("mab,mbc->mac", left, right, precision=lax.Precision.HIGHEST)

    c_real = (
        product(h_real, s_real)
        - product(h_imag, s_imag)
        - product(s_real, h_real)
        + product(s_imag, h_imag)
    )
    c_imag = (
        product(h_real, s_imag)
        + product(h_imag, s_real)
        - product(s_real, h_imag)
        - product(s_imag, h_real)
    )
    return jnp.stack([c_imag, -c_real]).reshape(2, count, NB * NB)


def self_energy(state, coupling, donors, counts):
    rounded = state.astype(jnp.bfloat16)
    padded = with_halo(rounded, (("ka", 1),), REACH * TILE)
    tiles_dev = coupling.shape[0]
    blocks = padded.reshape(2, tiles_dev + 2 * REACH, TILE, state.shape[2])
    total_tiles = tiles_dev * lax.axis_size("ka")
    local_tiles = jnp.arange(tiles_dev, dtype=jnp.int32)
    start_tile = lax.axis_index("ka") * tiles_dev
    offset = (donors - (start_tile + local_tiles)[:, None] + REACH) % total_tiles
    position = local_tiles[:, None] + offset
    picked = blocks[:, position]
    active = (jnp.arange(ND, dtype=jnp.int32)[None, :] < counts[:, None]).astype(jnp.bfloat16)
    masked = coupling * active[:, :, None, None]
    self_field = jnp.einsum("tskq,ctsqp->ctkp", masked, picked, preferred_element_type=jnp.float32)
    return -self_field.reshape(state.shape)


def local(density, h_bands, coupling, donors, counts):

    def bands_of(state, field):
        return (
            lax.all_to_all(state, "ba", split_axis=1, concat_axis=2, tiled=True),
            lax.all_to_all(field, "ba", split_axis=1, concat_axis=2, tiled=True),
        )

    def pairs_of(values):
        return lax.all_to_all(values, "ba", split_axis=2, concat_axis=1, tiled=True)

    half_step = 0.5 * step_size
    field_one = self_energy(density, coupling, donors, counts)
    state_band, field_band = bands_of(density, field_one)
    rate_one = commute(h_bands + field_band, state_band)
    middle = density + half_step * pairs_of(rate_one)
    field_two = self_energy(middle, coupling, donors, counts)
    middle_band, field_band_two = bands_of(middle, field_two)
    rate_two = commute(h_bands + field_band_two, middle_band)
    evolved = density + step_size * pairs_of(rate_two)
    return evolved


def solution(mesh):
    placed = (
        P(None, "ka", "ba"),
        P(None, ("ka", "ba"), None),
        P("ka", None, None, None),
        P("ka", None),
        P("ka"),
    )
    return jax.shard_map(
        local, mesh=mesh, in_specs=placed, out_specs=P(None, "ka", "ba"), check_vma=False
    )
```

profile of v0, /device:TPU:1, one launch (start us, length us, event | category | flops | bytes accessed | tf_op | source)
XLA Modules:
  0.0 243.6 jit_solution(3588705856673354187)
XLA Ops:
  0.0 1.1 convert_element_type.14
  1.1 13.7 %collective-permute-start.1 = (bf16[2,256,256]{2,1,0:T(8,128)(2,1)S(1)}, bf16[2,256,256]{2,1,0:T(8,128)(2,1)S(1)}, u32[]{:S(2)}, u32[]{:S(2)}) collective-permute-start(bf16[2,256,256]{2,1,0:T(8,128)(2,1)S(1)} %convert_element_type.14), channel_id=1, source_target_pairs={{16,0},{32,16},{48,32},{64,48},{80,64},{96,80},{112,96},{128,112},... | collective-permute-start | bytes 786440 | tf_op jit(solution)/shard_map/ppermute | solution.py:24
  14.8 1.9 collective-permute-start
  16.7 2.2 copy.114
  19.0 8.1 %all-to-all-start.1 = ((f32[2,256,256]{2,0,1:T(2,128)}), f32[2,256,256]{2,0,1:T(2,128)S(1)}, u32[]{:S(2)}, u32[]{:S(2)}) async-start(f32[2,256,256]{2,0,1:T(2,128)} %copy.114), calls=%async_computation.1 | async-start | bytes 1048576 | tf_op jit(solution)/shard_map/all_to_all | solution.py:77
  27.0 0.8 compare_select_fusion
  27.9 0.7 compare_convert_fusion
  29.7 1.2 copy.111
  30.9 13.3 %all-to-all-done.1 = f32[2,256,256]{2,0,1:T(2,128)S(1)} async-done(((f32[2,256,256]{2,0,1:T(2,128)}), f32[2,256,256]{2,0,1:T(2,128)S(1)}, u32[]{:S(2)}, u32[]{:S(2)}) %all-to-all-start.1) | async-done | bytes 524320 | tf_op jit(solution)/shard_map/all_to_all | solution.py:77
  44.2 3.5 %all-to-all-start = ((f32[2,256,256]{2,0,1:T(2,128)}), f32[2,256,256]{2,0,1:T(2,128)S(1)}, u32[]{:S(2)}, u32[]{:S(2)}) async-start(f32[2,256,256]{2,0,1:T(2,128)} %copy.111), calls=%async_computation | async-start | bytes 1048576 | tf_op jit(solution)/shard_map/all_to_all | solution.py:78
  48.4 16.1 %all-to-all-done = f32[2,256,256]{2,0,1:T(2,128)S(1)} async-done(((f32[2,256,256]{2,0,1:T(2,128)}), f32[2,256,256]{2,0,1:T(2,128)S(1)}, u32[]{:S(2)}, u32[]{:S(2)}) %all-to-all-start) | async-done | bytes 524320 | tf_op jit(solution)/shard_map/all_to_all | solution.py:78
  64.6 0.8 fusion.22
  66.8 1.4 convolution_bitcast_fusion.3
  68.2 1.4 fusion.24
  69.7 1.1 reshape_squeeze.26
  71.4 1.4 convolution_bitcast_fusion.5
  72.9 2.7 %fusion.7 = f32[16,64,64]{2,1,0:T(8,128)} fusion(f32[16,64,64]{2,1,0:T(8,128)S(1)} %convolution_bitcast_fusion.2, f32[16,64,64]{2,1,0:T(8,128)} %convolution_bitcast_fusion.3, f32[16,64,64]{2,1,0:T(8,128)} %fusion.24, f32[16,64,64]{2,1,0:T(8,128)S(1)} %reshape_squeeze.26, f32[16,64,64]{2,1,0:T(8,128)S(1)} %reshape_squeeze.25), kind=kOutput, calls=%fused_computation.20 | convolution fusion | flops 50593792 | bytes 1572864 | tf_op jit(solution)/shard_map/mab,mbc->mac/dot_general | solution.py:39
  75.5 1.9 stack.19
  77.5 1.7 fusion.9
  79.4 1.0 pad_maximum_fusion.2
  80.3 4.4 %copy.124 = f32[2,16,4096]{1,0,2:T(2,128)} copy(f32[2,16,4096]{2,1,0:T(8,128)S(1)} %pad_maximum_fusion.2) | data formatting | bytes 1048576 | tf_op jit(solution)/shard_map/stack | solution.py:53
  84.7 7.3 %reshape.87 = f32[16,1,8192]{2,1,0:T(1,128)S(1)} reshape(f32[4096,2,16]{2,1,0:T(2,128)} %bitcast.127) | data formatting | bytes 1048576
  92.0 20.0 %all_to_all.84 = f32[16,1,8192]{2,1,0:T(1,128)S(1)} all-to-all(f32[16,1,8192]{2,1,0:T(1,128)S(1)} %reshape.87), channel_id=1, replica_groups=mesh['ka'=32,'ba'=16] {'ba'}, dimensions={0} | all-to-all | bytes 1048576 | tf_op jit(solution)/shard_map/all_to_all | solution.py:82
  112.5 1.8 reduce
  114.3 6.9 %reshape.88 = f32[4096,2,16]{2,1,0:T(2,128)} reshape(f32[16,8192]{1,0:T(8,128)S(1)} %reduce) | data formatting | bytes 1048576
  121.3 5.6 %broadcast_multiply_fusion.1 = f32[2,16,4096]{1,0,2:T(2,128)} fusion(f32[4096,2,16]{2,1,0:T(2,128)} %reshape.88), kind=kLoop, calls=%fused_computation.3 | loop fusion | flops 131072 | bytes 1048576 | tf_op jit(solution)/shard_map/mul | solution.py:88
  126.8 5.2 %copy.125 = f32[2,16,16,256]{3,2,1,0:T(8,128)S(1)} copy(f32[2,16,16,256]{2,0,3,1:T(2,128)} %bitcast.129) | data formatting | bytes 1048576 | tf_op jit(solution)/shard_map/mul | solution.py:88
  132.1 1.2 copy.131
  133.3 4.1 %all-to-all-start.4 = ((f32[2,256,256]{2,0,1:T(2,128)}), f32[2,256,256]{2,0,1:T(2,128)}, u32[]{:S(2)}, u32[]{:S(2)}) async-start(f32[2,256,256]{2,0,1:T(2,128)} %copy.131), calls=%async_computation.4 | async-start | bytes 1048576 | tf_op jit(solution)/shard_map/all_to_all | solution.py:77
  137.5 7.0 %collective-permute-start.3 = (bf16[2,256,256]{2,1,0:T(8,128)(2,1)S(1)}, bf16[2,256,256]{2,1,0:T(8,128)(2,1)S(1)}, u32[]{:S(2)}, u32[]{:S(2)}) collective-permute-start(bf16[2,256,256]{2,1,0:T(8,128)(2,1)S(1)} %get-tuple-element.5), channel_id=1, source_target_pairs={{16,0},{32,16},{48,32},{64,48},{80,64},{96,80},{112,96},{128,112},... | collective-permute-start | bytes 786440 | tf_op jit(solution)/shard_map/ppermute | solution.py:24
  144.4 1.9 collective-permute-start.2
  146.4 3.6 %collective-permute-done.3 = bf16[2,256,256]{2,1,0:T(8,128)(2,1)S(1)} collective-permute-done((bf16[2,256,256]{2,1,0:T(8,128)(2,1)S(1)}, bf16[2,256,256]{2,1,0:T(8,128)(2,1)S(1)}, u32[]{:S(2)}, u32[]{:S(2)}) %collective-permute-start.3) | collective-permute-done | bytes 262176 | tf_op jit(solution)/shard_map/ppermute | solution.py:24
  150.0 7.4 %collective-permute-done.2 = bf16[2,256,256]{2,1,0:T(8,128)(2,1)S(1)} collective-permute-done((bf16[2,256,256]{2,1,0:T(8,128)(2,1)S(1)}, bf16[2,256,256]{2,1,0:T(8,128)(2,1)S(1)}, u32[]{:S(2)}, u32[]{:S(2)}) %collective-permute-start.2) | collective-permute-done | bytes 262176 | tf_op jit(solution)/shard_map/ppermute | solution.py:22
  158.5 1.2 copy.128
  159.7 6.6 %all-to-all-start.3 = ((f32[2,256,256]{2,0,1:T(2,128)}), f32[2,256,256]{2,0,1:T(2,128)S(1)}, u32[]{:S(2)}, u32[]{:S(2)}) async-start(f32[2,256,256]{2,0,1:T(2,128)} %copy.128), calls=%async_computation.3 | async-start | bytes 1048576 | tf_op jit(solution)/shard_map/all_to_all | solution.py:78
  166.3 1.3 copy.150
  168.0 15.5 %all-to-all-done.3 = f32[2,256,256]{2,0,1:T(2,128)S(1)} async-done(((f32[2,256,256]{2,0,1:T(2,128)}), f32[2,256,256]{2,0,1:T(2,128)S(1)}, u32[]{:S(2)}, u32[]{:S(2)}) %all-to-all-start.3) | async-done | bytes 524320 | tf_op jit(solution)/shard_map/all_to_all | solution.py:78
  184.2 0.6 fusion.26
  186.8 1.4 fusion.4
  188.2 1.2 stack.22
  191.6 4.4 %copy.133 = f32[2,16,4096]{1,0,2:T(2,128)} copy(f32[2,16,4096]{2,1,0:T(8,128)S(1)} %pad_maximum_fusion.3) | data formatting | bytes 1048576 | tf_op jit(solution)/shard_map/stack | solution.py:53
  196.0 7.3 %reshape.89 = f32[16,1,8192]{2,1,0:T(1,128)S(1)} reshape(f32[4096,2,16]{2,1,0:T(2,128)} %bitcast.128) | data formatting | bytes 1048576
  203.3 20.0 %all_to_all.85 = f32[16,1,8192]{2,1,0:T(1,128)S(1)} all-to-all(f32[16,1,8192]{2,1,0:T(1,128)S(1)} %reshape.89), channel_id=1, replica_groups=mesh['ka'=32,'ba'=16] {'ba'}, dimensions={0} | all-to-all | bytes 1048576 | tf_op jit(solution)/shard_map/all_to_all | solution.py:82
  223.3 1.8 reduce.1
  225.1 6.9 %reshape.90 = f32[4096,2,16]{2,1,0:T(2,128)} reshape(f32[16,8192]{1,0:T(8,128)S(1)} %reduce.1) | data formatting | bytes 1048576
  232.1 5.6 %broadcast_multiply_fusion = f32[2,16,4096]{1,0,2:T(2,128)} fusion(f32[4096,2,16]{2,1,0:T(2,128)} %reshape.90), kind=kLoop, calls=%fused_computation.2 | loop fusion | flops 131072 | bytes 1048576 | tf_op jit(solution)/shard_map/mul | solution.py:92
  237.6 5.1 %copy.134 = f32[2,16,16,256]{3,2,1,0:T(8,128)S(1)} copy(f32[2,16,16,256]{2,0,3,1:T(2,128)} %bitcast.130) | data formatting | bytes 1048576 | tf_op jit(solution)/shard_map/mul | solution.py:92
  242.7 0.9 bitcast_add_fusion
  (51 shorter events, 10.8 us)
Async XLA Ops:
  0.0 29.3 %copy-start.2 = (bf16[2,4,128,128]{3,2,1,0:T(8,128)(2,1)S(1)}, bf16[2,4,128,128]{3,2,1,0:T(8,128)(2,1)}, u32[]{:S(2)}) copy-start(bf16[2,4,128,128]{3,2,1,0:T(8,128)(2,1)} %param.7) | copy-start | bytes 786436
  1.1 27.5 %collective-permute-start.1 = (bf16[2,256,256]{2,1,0:T(8,128)(2,1)S(1)}, bf16[2,256,256]{2,1,0:T(8,128)(2,1)S(1)}, u32[]{:S(2)}, u32[]{:S(2)}) collective-permute-start(bf16[2,256,256]{2,1,0:T(8,128)(2,1)S(1)} %convert_element_type.14), channel_id=1, source_target_pairs={{16,0},{32,16},{48,32},{64,48},{80,64},{96,80},{112,96},{128,112},... | collective-permute-start | bytes 786440 | tf_op jit(solution)/shard_map/ppermute | solution.py:24
  14.8 13.8 %collective-permute-start = (bf16[2,256,256]{2,1,0:T(8,128)(2,1)S(1)}, bf16[2,256,256]{2,1,0:T(8,128)(2,1)S(1)}, u32[]{:S(2)}, u32[]{:S(2)}) collective-permute-start(bf16[2,256,256]{2,1,0:T(8,128)(2,1)S(1)} %convert_element_type.14), channel_id=1, source_target_pairs={{0,16},{16,32},{32,48},{48,64},{64,80},{80,96},{96,112},{112,128},... | collective-permute-start | bytes 786440 | tf_op jit(solution)/shard_map/ppermute | solution.py:22
  19.0 25.3 %all-to-all-start.1 = ((f32[2,256,256]{2,0,1:T(2,128)}), f32[2,256,256]{2,0,1:T(2,128)S(1)}, u32[]{:S(2)}, u32[]{:S(2)}) async-start(f32[2,256,256]{2,0,1:T(2,128)} %copy.114), calls=%async_computation.1 | async-start | bytes 1048576 | tf_op jit(solution)/shard_map/all_to_all | solution.py:77
  29.7 34.8 %copy-start.1 = (f32[2,16,4096]{2,1,0:T(8,128)S(1)}, f32[2,16,4096]{2,1,0:T(8,128)}, u32[]{:S(2)}) copy-start(f32[2,16,4096]{2,1,0:T(8,128)} %param.6) | copy-start | bytes 1572868
  44.2 20.2 %all-to-all-start = ((f32[2,256,256]{2,0,1:T(2,128)}), f32[2,256,256]{2,0,1:T(2,128)S(1)}, u32[]{:S(2)}, u32[]{:S(2)}) async-start(f32[2,256,256]{2,0,1:T(2,128)} %copy.111), calls=%async_computation | async-start | bytes 1048576 | tf_op jit(solution)/shard_map/all_to_all | solution.py:78
  126.8 5.2 %copy-start = (f32[2,256,256]{2,1,0:T(8,128)S(1)}, f32[2,256,256]{2,1,0:T(8,128)}, u32[]{:S(2)}) copy-start(f32[2,256,256]{2,1,0:T(8,128)} %param.5) | copy-start | bytes 1572868
  133.3 26.4 %all-to-all-start.4 = ((f32[2,256,256]{2,0,1:T(2,128)}), f32[2,256,256]{2,0,1:T(2,128)}, u32[]{:S(2)}, u32[]{:S(2)}) async-start(f32[2,256,256]{2,0,1:T(2,128)} %copy.131), calls=%async_computation.4 | async-start | bytes 1048576 | tf_op jit(solution)/shard_map/all_to_all | solution.py:77
  137.5 12.5 %collective-permute-start.3 = (bf16[2,256,256]{2,1,0:T(8,128)(2,1)S(1)}, bf16[2,256,256]{2,1,0:T(8,128)(2,1)S(1)}, u32[]{:S(2)}, u32[]{:S(2)}) collective-permute-start(bf16[2,256,256]{2,1,0:T(8,128)(2,1)S(1)} %get-tuple-element.5), channel_id=1, source_target_pairs={{16,0},{32,16},{48,32},{64,48},{80,64},{96,80},{112,96},{128,112},... | collective-permute-start | bytes 786440 | tf_op jit(solution)/shard_map/ppermute | solution.py:24
  144.4 13.0 %collective-permute-start.2 = (bf16[2,256,256]{2,1,0:T(8,128)(2,1)S(1)}, bf16[2,256,256]{2,1,0:T(8,128)(2,1)S(1)}, u32[]{:S(2)}, u32[]{:S(2)}) collective-permute-start(bf16[2,256,256]{2,1,0:T(8,128)(2,1)S(1)} %get-tuple-element.5), channel_id=1, source_target_pairs={{0,16},{16,32},{32,48},{48,64},{64,80},{80,96},{96,112},{112,128},... | collective-permute-start | bytes 786440 | tf_op jit(solution)/shard_map/ppermute | solution.py:22
  159.7 23.8 %all-to-all-start.3 = ((f32[2,256,256]{2,0,1:T(2,128)}), f32[2,256,256]{2,0,1:T(2,128)S(1)}, u32[]{:S(2)}, u32[]{:S(2)}) async-start(f32[2,256,256]{2,0,1:T(2,128)} %copy.128), calls=%async_computation.3 | async-start | bytes 1048576 | tf_op jit(solution)/shard_map/all_to_all | solution.py:78
where the time goes:
time: 245 us; the launch traced here: 244 us
  local copies, waits for them, and re-layouts  63.8 us (26%)
  waiting for transfers between devices  56 us (23%)
  starting transfers between devices  46.8 us (19%)
  blocking collectives  40 us (16%)
  other arithmetic  19.5 us (8%)
  matrix products  17.2 us (7%)
    all_to_all x2, blocking collectives, pairs_of(): return lax.all_to_all(values, 'ba', split_axis=2, concat_axis=1, tiled=True)  40 us
    all_to_all x2, waiting for transfers between devices, bands_of(): lax.all_to_all(field, 'ba', split_axis=1, concat_axis=2, tiled=True)  31.6 us
    unnamed x11, local copies, waits for them, and re-layouts  30.8 us
    ppermute x2, starting transfers between devices, with_halo(): lax.ppermute(head, axis, [((i + 1) % count, i) for i in range(count)])  20.6 us
    dot_general x16, matrix products, product(): jnp.einsum('mab,mbc->mac', left, right, precision=lax.Precision.HIGHEST)  16.5 us
    all_to_all x2, waiting for transfers between devices, bands_of(): lax.all_to_all(state, 'ba', split_axis=1, concat_axis=2, tiled=True)  13.3 us
    another operation x6, local copies, waits for them, and re-layouts, commute(): return jnp.stack([c_imag, -c_real]).reshape(2, count, NB * NB)  12.3 us
    all_to_all x2, starting transfers between devices, bands_of(): lax.all_to_all(state, 'ba', split_axis=1, concat_axis=2, tiled=True)  12.2 us
  transfers between devices with their start and end apart: 8, of which 5 were waited for; matrix products, arithmetic and copies ran while one was open for 4% of the time, Pallas kernels for 0%

commit v1 on v0

v1 whole, which is shorter than its diff:
```python
import functools

import jax
import jax.numpy as jnp
from jax import lax
from jax.experimental import pallas as pl
from jax.experimental.pallas import tpu as pltpu
from jax.sharding import PartitionSpec as P

NB = 64
TILE = 128
ND = 4
REACH = 2
TILES = 64
GROUP = 16
ROWS = 64
MESH = pl.DeviceIdType.MESH
F32, BF16, I16 = jnp.float32, jnp.bfloat16, jnp.int16
TOP = 32760.0

step_size = 0.25


def low_half(shape):
    return lax.broadcasted_iota(jnp.int32, shape, len(shape) - 1) < NB


def merge(real, imag):
    low = low_half(real.shape)
    first = jnp.where(low, real, pltpu.roll(imag, NB, 1))
    second = jnp.where(low, pltpu.roll(real, NB, 1), imag)
    return first, second


def split(first, second):
    low = low_half(first.shape)
    real = jnp.where(low, first, pltpu.roll(second, NB, 1))
    imag = jnp.where(low, pltpu.roll(first, NB, 1), second)
    return real, imag


def encode(values):
    top = jnp.max(jnp.abs(values), axis=0, keepdims=True)
    top = jnp.maximum(top, 1e-30)
    codes = jnp.round(values * (TOP / top)).astype(jnp.int32).astype(I16)
    return codes, top * (1.0 / TOP)


def decode(codes, scale):
    return codes.astype(jnp.int32).astype(F32) * scale


def halves(values):
    high = values.astype(BF16)
    return high, (values - high.astype(F32)).astype(BF16)


def rate(hamilton, state):
    sign = jnp.where(low_half(state.shape), 1.0, -1.0).astype(F32)
    turned_s = pltpu.roll(state, NB, 1) * sign
    turned_h = pltpu.roll(hamilton, NB, 1) * sign
    right_high, right_low = halves(
        jnp.concatenate([turned_s, state, turned_h, hamilton], axis=0)
    )
    left_high, left_low = halves(jnp.concatenate([hamilton, -state], axis=1))
    left = jnp.concatenate([left_high, left_low], axis=0)
    right = jnp.concatenate([right_high, right_low], axis=1)
    out = jnp.dot(left, right, preferred_element_type=F32)
    return out[:NB, :TILE] + (out[:NB, TILE:] + out[NB:, :TILE])


def kernel(
    dens_hbm, h_hbm, coup_hbm, donors, counts, out_hbm,
    dens, hraw, coup, low0, halo0, mix, hband, state, ham, rate_two, sigma,
    enc_s, enc_r, scale_s, scale_r, mid_s, mid_r, halo1, out_v,
    load_sem, out_sem, enc_ss, enc_rs, scale_ss, scale_rs,
    mid_ss, mid_rs, halo0_ss, halo0_rs, halo1_ss, halo1_rs,
):
    me = lax.axis_index("ba")
    mine = lax.axis_index("ka")
    ring = lax.axis_size("ka")
    sides = (lax.rem(mine + 1, ring), lax.rem(mine + ring - 1, ring))

    loads = [
        pltpu.make_async_copy(a, b, load_sem.at[i])
        for i, (a, b) in enumerate(((dens_hbm, dens), (coup_hbm, coup), (h_hbm, hraw)))
    ]
    for load in loads:
        load.start()

    barrier = pltpu.get_barrier_semaphore()
    for i in range(1, GROUP):
        pl.semaphore_signal(
            barrier, inc=1, device_id={"ba": lax.rem(me + i, GROUP)}, device_id_type=MESH
        )
    for side in sides:
        pl.semaphore_signal(barrier, inc=1, device_id={"ka": side}, device_id_type=MESH)

    loads[0].wait()
    for t in range(2):
        cut = pl.ds(t * TILE, TILE)
        first, second = merge(dens[0, :, cut], dens[1, :, cut])
        low0[2 * t] = first.astype(BF16)
        low0[2 * t + 1] = second.astype(BF16)
        sigma[2 * t] = first
        sigma[2 * t + 1] = second

    pl.semaphore_wait(barrier, GROUP + 1)

    def halo0_copy(side):
        return pltpu.make_async_remote_copy(
            src_ref=low0,
            dst_ref=halo0.at[side],
            send_sem=halo0_ss.at[side],
            recv_sem=halo0_rs.at[side],
            device_id={"ka": sides[side]},
            device_id_type=MESH,
        )

    for side in range(2):
        halo0_copy(side).start()

    def enc_copy(phase, there, slot_s, slot_r):
        return pltpu.make_async_remote_copy(
            src_ref=enc_s.at[phase, slot_s],
            dst_ref=enc_r.at[phase, slot_r],
            send_sem=enc_ss.at[phase, slot_s],
            recv_sem=enc_rs.at[phase, slot_r],
            device_id={"ba": there},
            device_id_type=MESH,
        )

    def scale_copy(phase, there, slot_s, slot_r):
        return pltpu.make_async_remote_copy(
            src_ref=scale_s.at[phase, slot_s],
            dst_ref=scale_r.at[phase, slot_r],
            send_sem=scale_ss.at[phase, slot_s],
            recv_sem=scale_rs.at[phase, slot_r],
            device_id={"ba": there},
            device_id_type=MESH,
        )

    def send_all(phase, values_of):
        def step(i, carry):
            there = lax.rem(me + i, GROUP)
            codes, scale = encode(values_of(there))
            enc_s[phase, there] = codes
            scale_s[phase, there] = scale
            enc_copy(phase, there, there, me).start()
            scale_copy(phase, there, there, me).start()
            return carry

        lax.fori_loop(1, GROUP, step, 0)
        codes, scale = encode(values_of(me))
        enc_r[phase, me] = codes
        scale_r[phase, me] = scale

    def wait_from(phase, i):
        @pl.when(i > 0)
        def _():
            src = lax.rem(me + GROUP - i, GROUP)
            enc_copy(phase, src, src, src).wait_recv()
            scale_copy(phase, src, src, src).wait_recv()

    def momenta(block):
        return pl.ds(pl.multiple_of(block * GROUP, GROUP), GROUP)

    def rows(block):
        return pl.ds(pl.multiple_of(block * ROWS, ROWS), ROWS)

    def of_momenta(block):
        return sigma[:, momenta(block), :].reshape(ROWS, TILE)

    send_all(0, of_momenta)

    loads[1].wait()
    for t in range(2):
        tile = mine * 2 + t
        for position in range(2 + 2 * REACH):
            block = jnp.zeros((TILE, TILE), F32)
            if 0 <= position - t <= 2 * REACH:
                for s in range(ND):
                    offset = lax.rem(donors[t, s] - tile + REACH + TILES, TILES)
                    used = jnp.logical_and(offset == position - t, counts[t] > s)
                    weight = jnp.where(used, -1.0, 0.0).astype(F32)
                    block = block + coup[t, s].astype(F32) * weight
            mix[pl.ds(t * TILE, TILE), pl.ds(position * TILE, TILE)] = block.astype(BF16)

    loads[2].wait()

    def lay(t, carry):
        cut = pl.ds(pl.multiple_of(t * TILE, TILE), TILE)
        first, second = merge(hraw[0, :, cut], hraw[1, :, cut])
        base = pl.multiple_of(t * 2 * GROUP, 2 * GROUP)
        hband[pl.ds(base, GROUP), :] = first
        hband[pl.ds(base + GROUP, GROUP), :] = second
        return carry

    lax.fori_loop(0, NB // 2, lay, 0)

    def field(left, own, right):
        for a in range(4):
            total = jnp.zeros((2 * TILE, TILE), F32)
            for i, part in enumerate((left(a), own(a), right(a))):
                total += jnp.dot(
                    mix[:, pl.ds(i * 2 * TILE, 2 * TILE)], part, preferred_element_type=F32
                )
            sigma[a] = total

    for side in range(2):
        halo0_copy(side).wait_recv()
    field(lambda a: halo0[0, a], lambda a: low0[a], lambda a: halo0[1, a])
    send_all(1, of_momenta)

    def take_state(i, carry):
        wait_from(0, i)
        src = lax.rem(me + GROUP - i, GROUP)
        state[rows(src), :] = decode(enc_r[0, src], scale_r[0, src])
        return carry

    lax.fori_loop(0, GROUP, take_state, 0)

    def take_field(phase):
        def step(i, carry):
            wait_from(phase, i)
            src = lax.rem(me + GROUP - i, GROUP)
            ham[rows(src), :] = hband[rows(src), :] + decode(
                enc_r[phase, src], scale_r[phase, src]
            )
            return carry

        lax.fori_loop(0, GROUP, step, 0)

    take_field(1)

    def first_stage(m, carry):
        cut = pl.ds(m, NB, stride=GROUP)
        here = state[cut, :]
        state[cut, :] = here + (0.5 * step_size) * rate(ham[cut, :], here)
        return carry

    lax.fori_loop(0, GROUP, first_stage, 0)

    def mid_copy(there, slot_s, slot_r):
        return pltpu.make_async_remote_copy(
            src_ref=mid_s.at[slot_s],
            dst_ref=mid_r.at[slot_r],
            send_sem=mid_ss.at[slot_s],
            recv_sem=mid_rs.at[slot_r],
            device_id={"ba": there},
            device_id_type=MESH,
        )

    def send_mid(i, carry):
        there = lax.rem(me + i, GROUP)
        mid_s[there] = state[rows(there), :].astype(BF16)
        mid_copy(there, there, me).start()
        return carry

    lax.fori_loop(1, GROUP, send_mid, 0)
    mid_r[me] = state[rows(me), :].astype(BF16)

    def halo1_copy(side, slot):
        return pltpu.make_async_remote_copy(
            src_ref=mid_r.at[slot],
            dst_ref=halo1.at[side, slot],
            send_sem=halo1_ss.at[side, slot],
            recv_sem=halo1_rs.at[side, slot],
            device_id={"ka": sides[side]},
            device_id_type=MESH,
        )

    def forward(i, carry):
        src = lax.rem(me + GROUP - i, GROUP)

        @pl.when(i > 0)
        def _():
            mid_copy(src, src, src).wait_recv()

        for side in range(2):
            halo1_copy(side, src).start()
        return carry

    lax.fori_loop(0, GROUP, forward, 0)

    def halo1_in(i, carry):
        for side in range(2):
            halo1_copy(side, i).wait_recv()
        return carry

    lax.fori_loop(0, GROUP, halo1_in, 0)

    def band(ref, a):
        return ref[:, pl.ds(a * GROUP, GROUP), :].reshape(2 * TILE, TILE)

    field(
        lambda a: band(halo1.at[0], a), lambda a: band(mid_r, a), lambda a: band(halo1.at[1], a)
    )
    send_all(2, of_momenta)
    take_field(2)

    def second_stage(m, carry):
        cut = pl.ds(m, NB, stride=GROUP)
        rate_two[cut, :] = step_size * rate(ham[cut, :], state[cut, :])
        return carry

    lax.fori_loop(0, GROUP, second_stage, 0)
    send_all(3, lambda block: rate_two[rows(block), :])

    def out_copy(src):
        return pltpu.make_async_copy(
            out_v.at[:, momenta(src), :], out_hbm.at[:, momenta(src), :], out_sem.at[src]
        )

    def finish(i, carry):
        wait_from(3, i)
        src = lax.rem(me + GROUP - i, GROUP)
        change = decode(enc_r[3, src], scale_r[3, src])
        for t in range(2):
            base = t * 2 * GROUP
            real, imag = split(change[base : base + GROUP], change[base + GROUP : base + 2 * GROUP])
            cut = pl.ds(t * TILE, TILE)
            out_v[0, momenta(src), cut] = dens[0, momenta(src), cut] + real
            out_v[1, momenta(src), cut] = dens[1, momenta(src), cut] + imag
        out_copy(src).start()
        return carry

    lax.fori_loop(0, GROUP, finish, 0)

    for side in range(2):
        halo0_copy(side).wait_send()

    def drain(i, carry):
        there = lax.rem(me + i, GROUP)
        for phase in range(4):
            enc_copy(phase, there, there, me).wait_send()
            scale_copy(phase, there, there, me).wait_send()
        mid_copy(there, there, me).wait_send()
        return carry

    lax.fori_loop(1, GROUP, drain, 0)

    def drain_all(i, carry):
        for side in range(2):
            halo1_copy(side, i).wait_send()
        out_copy(i).wait()
        return carry

    lax.fori_loop(0, GROUP, drain_all, 0)


def local(density, h_bands, coupling, donors, counts):
    message = (GROUP, ROWS, TILE)
    big = (NB * GROUP, TILE)
    dma = pltpu.SemaphoreType.DMA
    anywhere = pl.BlockSpec(memory_space=pl.ANY)
    scalars = pl.BlockSpec(memory_space=pltpu.SMEM)
    return pl.pallas_call(
        kernel,
        out_shape=jax.ShapeDtypeStruct(density.shape, F32),
        in_specs=[anywhere, anywhere, anywhere, scalars, scalars],
        out_specs=anywhere,
        scratch_shapes=[
            pltpu.VMEM(density.shape, F32),
            pltpu.VMEM(h_bands.shape, F32),
            pltpu.VMEM(coupling.shape, BF16),
            pltpu.VMEM((4, 2 * TILE, TILE), BF16),
            pltpu.VMEM((2, 4, 2 * TILE, TILE), BF16),
            pltpu.VMEM((2 * TILE, 6 * TILE), BF16),
            pltpu.VMEM(big, F32),
            pltpu.VMEM(big, F32),
            pltpu.VMEM(big, F32),
            pltpu.VMEM(big, F32),
            pltpu.VMEM((4, 2 * TILE, TILE), F32),
            pltpu.VMEM((4, *message), I16),
            pltpu.VMEM((4, *message), I16),
            pltpu.VMEM((4, GROUP, 1, TILE), F32),
            pltpu.VMEM((4, GROUP, 1, TILE), F32),
            pltpu.VMEM(message, BF16),
            pltpu.VMEM(message, BF16),
            pltpu.VMEM((2, *message), BF16),
            pltpu.VMEM(density.shape, F32),
            dma((3,)),
            dma((GROUP,)),
            dma((4, GROUP)),
            dma((4, GROUP)),
            dma((4, GROUP)),
            dma((4, GROUP)),
            dma((GROUP,)),
            dma((GROUP,)),
            dma((2,)),
            dma((2,)),
            dma((2, GROUP)),
            dma((2, GROUP)),
        ],
        compiler_params=pltpu.CompilerParams(
            collective_id=0, has_side_effects=True, vmem_limit_bytes=40 << 20
        ),
    )(density, h_bands, coupling, donors, counts)


def solution(mesh):
    placed = (
        P(None, "ka", "ba"),
        P(None, ("ka", "ba"), None),
        P("ka", None, None, None),
        P("ka", None),
        P("ka"),
    )
    return jax.shard_map(
        local, mesh=mesh, in_specs=placed, out_specs=P(None, "ka", "ba"), check_vma=False
    )
```

time: 245 us -> 86.1 us (0.35)
  Pallas kernels: 0 us -> 80.7 us
  local copies, waits for them, and re-layouts: 63.8 us -> 5.16 us
  waiting for transfers between devices: 56 us -> 0 us
  starting transfers between devices: 46.8 us -> 0 us
  blocking collectives: 40 us -> 0 us
  other arithmetic: 19.5 us -> 0 us
  matrix products: 17.2 us -> 0 us
    pallas_call x0 -> x1, Pallas kernels: none -> 80.7 us  [local(): pl.pallas_call(kernel, out_shape=jax.ShapeDtypeStruct(density.shape, F32)...]
    all_to_all x4 -> x0, waiting for transfers between devices: 44.9 us -> none  [the longest x2 31.6 us: bands_of(): lax.all_to_all(field, 'ba', split_axis=1, concat_axis=2, tiled=True)]
    all_to_all x2 -> x0, blocking collectives: 40 us -> none  [pairs_of(): return lax.all_to_all(values, 'ba', split_axis=2, concat_axis=1, tiled=True)]
    unnamed x11, local copies, waits for them, and re-layouts: 30.8 us -> 5.16 us
    ppermute x4 -> x0, starting transfers between devices: 24.5 us -> none  [the longest x2 20.6 us: with_halo(): lax.ppermute(head, axis, [((i + 1) % count, i) for i in range(count)])]
    all_to_all x4 -> x0, starting transfers between devices: 22.3 us -> none  [the longest x2 12.2 us: bands_of(): lax.all_to_all(state, 'ba', split_axis=1, concat_axis=2, tiled=True)]
    dot_general x18 -> x0, matrix products: 17.2 us -> none  [the longest x16 16.5 us: product(): jnp.einsum('mab,mbc->mac', left, right, precision=lax.Precision.HIGHEST)]
    another operation x14 -> x0, local copies, waits for them, and re-layouts: 14.6 us -> none  [the longest x6 12.3 us: commute(): return jnp.stack([c_imag, -c_real]).reshape(2, count, NB * NB)]
  transfers between devices with their start and end apart: 8 -> 0, of which waited for: 5 -> 0; matrix products, arithmetic and copies ran while one was open for 4% -> 0% of each run, Pallas kernels for 0% -> 0%
where the time goes in v1:
time: 86.1 us; the launch traced here: 85.9 us
  Pallas kernels  80.7 us (94%)
  local copies, waits for them, and re-layouts  5.16 us (6%)
    pallas_call x1, Pallas kernels, local(): pl.pallas_call(kernel, out_shape=jax.ShapeDtypeStruct(density.shape, F32)...  80.7 us
    unnamed x11, local copies, waits for them, and re-layouts  5.16 us

profile of v1, /device:TPU:1, one launch (start us, length us, event | category | flops | bytes accessed | tf_op | source)
XLA Modules:
  0.0 85.9 jit_solution(5516847631828973072)
XLA Ops:
  0.0 0.0 copy-start
  0.0 1.0 %copy-done = f32[2,256,256]{2,1,0:T(8,128)S(1)} copy-done((f32[2,256,256]{2,1,0:T(8,128)S(1)}, f32[2,256,256]{2,1,0:T(8,128)}, u32[]{:S(2)}) %copy-start) | copy-done | bytes 524312
  1.0 0.0 copy-start.1
  1.0 1.0 %copy-done.1 = f32[2,16,4096]{2,1,0:T(8,128)S(1)} copy-done((f32[2,16,4096]{2,1,0:T(8,128)S(1)}, f32[2,16,4096]{2,1,0:T(8,128)}, u32[]{:S(2)}) %copy-start.1) | copy-done | bytes 524312
  2.1 0.0 copy-start.2
  2.1 0.9 %copy-done.2 = bf16[2,4,128,128]{3,2,1,0:T(8,128)(2,1)S(1)} copy-done((bf16[2,4,128,128]{3,2,1,0:T(8,128)(2,1)S(1)}, bf16[2,4,128,128]{3,2,1,0:T(8,128)(2,1)}, u32[]{:S(2)}) %copy-start.2) | copy-done | bytes 262168
  3.0 0.0 copy-start.3
  3.0 0.7 copy-done.3
  3.7 0.0 copy-start.4
  3.7 0.7 copy-done.4
  4.4 80.7 %shard_map.55 = f32[2,256,256]{2,1,0:T(8,128)S(1)} custom-call(f32[2,256,256]{2,1,0:T(8,128)S(1)} %copy-done, f32[2,16,4096]{2,1,0:T(8,128)S(1)} %copy-done.1, bf16[2,4,128,128]{3,2,1,0:T(8,128)(2,1)S(1)} %copy-done.2, s32[2,4]{1,0:T(2,128)S(1)} %copy-done.3, s32[2]{0:T(128)S(1)} %copy-done.4), custom_call_target="tpu_custom_call" | custom-call | tf_op jit(solution)/shard_map/pallas_call | solution.py:358
  85.1 0.8 copy.7
Async XLA Ops:
  0.0 1.0 %copy-start = (f32[2,256,256]{2,1,0:T(8,128)S(1)}, f32[2,256,256]{2,1,0:T(8,128)}, u32[]{:S(2)}) copy-start(f32[2,256,256]{2,1,0:T(8,128)} %dens_hbm.1) | copy-start | bytes 1572868
  1.0 1.0 %copy-start.1 = (f32[2,16,4096]{2,1,0:T(8,128)S(1)}, f32[2,16,4096]{2,1,0:T(8,128)}, u32[]{:S(2)}) copy-start(f32[2,16,4096]{2,1,0:T(8,128)} %h_hbm.1) | copy-start | bytes 1572868
  2.1 0.9 %copy-start.2 = (bf16[2,4,128,128]{3,2,1,0:T(8,128)(2,1)S(1)}, bf16[2,4,128,128]{3,2,1,0:T(8,128)(2,1)}, u32[]{:S(2)}) copy-start(bf16[2,4,128,128]{3,2,1,0:T(8,128)(2,1)} %coup_hbm.1) | copy-start | bytes 786436
  3.0 0.7 copy-start.3
  3.7 0.7 copy-start.4
